TPU v7x, 32 devices: a whole 2x2x4 slice. The times are simulated.
32 devices in a mesh: pipe: 4 (over x, core), sp: 2 (over y), dp: 4 (over z).
Axes of the slice: x: 2, y: 2, z: 4, core: 2. Of those that a mesh axis runs over, the one named last changes fastest.
Arguments:
- fresh_input: bfloat16 [4, 4, 120, 240, 128], P('pipe', 'dp', 'sp'), may hold values from -6 to 6
- saved_input: bfloat16 [4, 4, 120, 240, 128], P('pipe', 'dp', 'sp'), may hold values from -6 to 6
- output_grad: bfloat16 [4, 4, 120, 240, 128], P('pipe', 'dp', 'sp'), may hold values from -6 to 6
- expand_weight: bfloat16 [4, 128, 768], P('pipe'), may hold values from -0.5 to 0.5
- reduce_weight: bfloat16 [4, 768, 128], P('pipe'), may hold values from -0.21875 to 0.21875
- filter_weight: float32 [4, 2, 120, 128], P('pipe'), may hold values from -6 to 6
- cycle_table: int32 [120], replicated, may hold values from 0 to 119, each once
Outputs:
- next_input: bfloat16 [4, 4, 120, 240, 128], P('pipe', 'dp', 'sp')
- input_grad: bfloat16 [4, 4, 120, 240, 128], P('pipe', 'dp', 'sp')
- expand_grad: float32 [4, 128, 768], P('pipe', None, 'dp')
- reduce_grad: float32 [4, 768, 128], P('pipe', 'dp')
- filter_grad: float32 [4, 2, 120, 128], P('pipe')
Inputs may be any that keep to these rules, and one draw needn't show every extreme that they name: `cycle_table`: each of 0 .. 119 appears once; values 120 or more mark empty cycle slots.
All inputs are finite; a program needn't handle non-finite values.
Results may differ from a plain program's by a relative error of at most 0.025.
Values may be sent and summed in bfloat16 or wider, within the bound.
A program may use at most 192 MiB of HBM per device.

v0:
```python
import math
import jax
import jax.numpy as jnp
from jax import lax
from jax.sharding import PartitionSpec as P

NLAT = 120
NLON = 240
ROOT_HALF = 0.7071067811865476
INV_ROOT_TAU = 0.3989422804014327


def from_behind(block, axis, distance):
    devices = range(lax.axis_size(axis))
    route = [(i - distance, i) for i in devices if i - distance in devices]
    return lax.ppermute(block, axis, route)


def gelu_value(pre_act):
    return 0.5 * pre_act * (1.0 + lax.erf(pre_act * ROOT_HALF))


def gelu_slope(pre_act):
    return (
        0.5 * (1.0 + lax.erf(pre_act * ROOT_HALF))
        + pre_act * jnp.exp(-0.5 * pre_act * pre_act) * INV_ROOT_TAU
    )


def legendre(lat_index, order_index, cycles):
    lat_ok = (lat_index < cycles).astype(jnp.float32)
    order_ok = (order_index < cycles).astype(jnp.float32)
    colatitude = math.pi * (jnp.minimum(lat_index, cycles - 1).astype(jnp.float32) + 0.5) / cycles
    cosine = jnp.cos(colatitude)[None, :]
    sine_value = jnp.sin(colatitude)[None, :]
    order_value = jnp.minimum(order_index, cycles - 1).astype(jnp.float32)[:, None]
    log_start = 0.5 * (
        jnp.log((2.0 * order_value + 1.0) / (4.0 * math.pi))
        + lax.lgamma(2.0 * order_value + 1.0)
        - 2.0 * lax.lgamma(order_value + 1.0)
        - order_value * math.log(4.0)
    ) + order_value * jnp.log(sine_value)
    starting = jnp.exp(log_start)
    zero_rows = jnp.zeros_like(starting)

    def advance(state_pair, degree):
        previous, earlier = state_pair
        degree_value = degree.astype(jnp.float32)
        upper_term = jnp.maximum(4.0 * degree_value * degree_value - 1.0, 0.0)
        ratio_main = jnp.sqrt(
            upper_term / jnp.maximum(degree_value * degree_value - order_value * order_value, 1.0)
        )
        ratio_back = jnp.sqrt(
            jnp.maximum((degree_value - 1.0) ** 2 - order_value * order_value, 0.0)
            / jnp.maximum(4.0 * (degree_value - 1.0) ** 2 - 1.0, 1.0)
        )
        rising = ratio_main * (cosine * previous - ratio_back * earlier)
        current = jnp.where(
            degree_value == order_value,
            starting,
            jnp.where(degree_value > order_value, rising, 0.0),
        )
        return ((current, previous), current)

    _, stacked = lax.scan(advance, (zero_rows, zero_rows), jnp.arange(cycles, dtype=jnp.int32))
    valid_mask = order_ok[:, None] * lat_ok[None, :]
    return jnp.transpose(stacked, (1, 0, 2)) * valid_mask[:, None, :]


def cycle_weights(lat_index, cycles):
    valid_cycle = (lat_index < cycles).astype(jnp.float32)
    colatitude = math.pi * (jnp.minimum(lat_index, cycles - 1).astype(jnp.float32) + 0.5) / cycles
    return math.pi / cycles * jnp.sin(colatitude) * valid_cycle


def fourier_tables(order_index, cycles, points):
    valid_order = (order_index < cycles).astype(jnp.float32)[None, :]
    order_value = jnp.minimum(order_index, cycles - 1)
    longitude = jnp.arange(points, dtype=jnp.int32)
    phase_angle = (
        2.0
        * math.pi
        / points
        * (longitude[:, None] * order_value[None, :] % points).astype(jnp.float32)
    )
    scaled = valid_order * (2.0 * math.pi / points)
    forward = jnp.concatenate(
        [jnp.cos(phase_angle) * scaled, -jnp.sin(phase_angle) * scaled], axis=1
    )
    order_scale = jnp.where(order_value == 0, 1.0, 2.0)[None, :] * valid_order / (2.0 * math.pi)
    inverse = jnp.concatenate(
        [jnp.cos(phase_angle) * order_scale, -jnp.sin(phase_angle) * order_scale], axis=1
    ).T
    return (forward.astype(jnp.bfloat16), inverse.astype(jnp.bfloat16))


def joint_orders(coeffs):
    return lax.all_to_all(coeffs, "sp", split_axis=3, concat_axis=1, tiled=True)


def joint_cycles(values):
    return lax.all_to_all(values, "sp", split_axis=1, concat_axis=3, tiled=True)


def spectral_pass(tokens, filt, forward, analysis, synthesis, inverse, to_orders, to_cycles):
    batch_count, row_count, points, chan_count = tokens.shape
    order_count = forward.shape[1] // 2
    coeffs = jnp.einsum(
        "sjnc,nk->sjkc", tokens, forward, preferred_element_type=jnp.float32
    ).astype(jnp.bfloat16)
    coeffs = coeffs.reshape(batch_count, row_count, 2, order_count, chan_count)
    arrived = to_orders(coeffs)
    spectra = jnp.einsum("tlj,sjrtc->strlc", analysis, arrived, preferred_element_type=jnp.float32)
    real_part = filt[0] * spectra[:, :, 0] - filt[1] * spectra[:, :, 1]
    imag_part = filt[0] * spectra[:, :, 1] + filt[1] * spectra[:, :, 0]
    filtered = jnp.stack([real_part, imag_part], axis=2).astype(jnp.bfloat16)
    values = jnp.einsum(
        "tlj,strlc->sjrtc", synthesis, filtered, preferred_element_type=jnp.float32
    ).astype(jnp.bfloat16)
    returned = to_cycles(values).reshape(batch_count, row_count, 2 * order_count, chan_count)
    spatial = jnp.einsum("sjkc,kn->sjnc", returned, inverse, preferred_element_type=jnp.float32)
    return (spatial, spectra)


def mlp_pass(tokens, spatial, expand, contract, cycle_mask):
    grid_shape = tokens.shape
    flat_rows = (tokens.astype(jnp.float32) + spatial).reshape(-1, grid_shape[-1])
    mixed_b = flat_rows.astype(jnp.bfloat16)
    hidden_pre = jnp.dot(mixed_b, expand, preferred_element_type=jnp.float32)
    hidden = gelu_value(hidden_pre).astype(jnp.bfloat16)
    result = flat_rows + jnp.dot(hidden, contract, preferred_element_type=jnp.float32)
    result = (result.reshape(grid_shape) * cycle_mask[:, None, None]).astype(jnp.bfloat16)
    return (result, mixed_b, hidden_pre, hidden)


def backward_rows(cotangent, cycle_mask, mixed_b, hidden_pre, hidden, expand, contract):
    chan_count = cotangent.shape[-1]
    masked = (cotangent * cycle_mask.astype(jnp.bfloat16)[:, None, None]).reshape(-1, chan_count)
    grad_reduce = jnp.dot(hidden.T, masked, preferred_element_type=jnp.float32)
    grad_hidden = jnp.dot(masked, contract.T, preferred_element_type=jnp.float32)
    grad_pre = (grad_hidden * gelu_slope(hidden_pre)).astype(jnp.bfloat16)
    grad_expand = jnp.dot(mixed_b.T, grad_pre, preferred_element_type=jnp.float32)
    grad_mixed = masked.astype(jnp.float32) + jnp.dot(
        grad_pre, expand.T, preferred_element_type=jnp.float32
    )
    return (grad_mixed, grad_expand, grad_reduce)


def on_device(
    fresh_input, saved_input, output_grad, expand_weight, reduce_weight, filter_weight, cycle_table
):
    slot_count = fresh_input.shape[2]
    position = lax.axis_index("sp")
    order_table = jnp.arange(slot_count * lax.axis_size("sp"), dtype=jnp.int32)
    own_cycles = lax.dynamic_slice_in_dim(cycle_table, position * slot_count, slot_count)
    own_orders = lax.dynamic_slice_in_dim(order_table, position * slot_count, slot_count)
    cycle_mask = (own_cycles < NLAT).astype(jnp.float32)
    table = legendre(cycle_table, own_orders, NLAT)
    analysis = (table * cycle_weights(cycle_table, NLAT)[None, None, :]).astype(jnp.bfloat16)
    synthesis = table.astype(jnp.bfloat16)
    forward, inverse = fourier_tables(order_table, NLAT, NLON)
    filt = filter_weight[0]
    expand = expand_weight[0]
    contract = reduce_weight[0]
    fresh = fresh_input[0, 0]
    saved = saved_input[0, 0]
    spatial, spectra = spectral_pass(
        jnp.stack([fresh, saved]),
        filt,
        forward,
        analysis,
        synthesis,
        inverse,
        joint_orders,
        joint_cycles,
    )
    fresh_spatial = spatial[0]
    saved_spatial = spatial[1]
    saved_spectra = spectra[1]
    block = mlp_pass(fresh, fresh_spatial, expand, contract, cycle_mask)[0]
    next_input = from_behind(block[None, None], "pipe", 1)
    _, mixed_b, hidden_pre, hidden = mlp_pass(saved, saved_spatial, expand, contract, cycle_mask)
    grad_mixed, grad_expand, grad_reduce = backward_rows(
        output_grad[0, 0], cycle_mask, mixed_b, hidden_pre, hidden, expand, contract
    )
    grid_shape = saved.shape
    row_count, points, chan_count = grid_shape
    order_count = forward.shape[1] // 2
    grad_rows = grad_mixed.reshape(grid_shape).astype(jnp.bfloat16)
    grad_values = jnp.einsum(
        "jnc,kn->jkc", grad_rows, inverse, preferred_element_type=jnp.float32
    ).astype(jnp.bfloat16)
    grad_values = grad_values.reshape(row_count, 2, order_count, chan_count)
    arrived = lax.all_to_all(grad_values, "sp", split_axis=2, concat_axis=0, tiled=True)
    grad_filtered = jnp.einsum(
        "tlj,jrtc->trlc", synthesis, arrived, preferred_element_type=jnp.float32
    )
    filter_real = jnp.sum(
        grad_filtered[:, 0] * saved_spectra[:, 0] + grad_filtered[:, 1] * saved_spectra[:, 1],
        axis=0,
    )
    filter_imag = jnp.sum(
        grad_filtered[:, 1] * saved_spectra[:, 0] - grad_filtered[:, 0] * saved_spectra[:, 1],
        axis=0,
    )
    grad_spectra = jnp.stack(
        [
            filt[0] * grad_filtered[:, 0] + filt[1] * grad_filtered[:, 1],
            filt[0] * grad_filtered[:, 1] - filt[1] * grad_filtered[:, 0],
        ],
        axis=1,
    ).astype(jnp.bfloat16)
    grad_coeffs = jnp.einsum(
        "tlj,trlc->jrtc", analysis, grad_spectra, preferred_element_type=jnp.float32
    ).astype(jnp.bfloat16)
    returned = lax.all_to_all(grad_coeffs, "sp", split_axis=0, concat_axis=2, tiled=True)
    grad_tokens = jnp.einsum(
        "jkc,nk->jnc",
        returned.reshape(row_count, 2 * order_count, chan_count),
        forward,
        preferred_element_type=jnp.float32,
    )
    input_grad = (
        (grad_mixed.reshape(grid_shape) + grad_tokens) * cycle_mask[:, None, None]
    ).astype(jnp.bfloat16)
    sent_back = from_behind(input_grad[None, None], "pipe", -1)
    filter_grad = lax.psum(jnp.stack([filter_real, filter_imag]), ("sp", "dp"))
    summed = (
        lax.psum(grad_expand.astype(jnp.bfloat16), "sp").astype(jnp.float32),
        lax.psum(grad_reduce.astype(jnp.bfloat16), "sp").astype(jnp.float32),
    )
    expand_grad, reduce_grad = (
        lax.psum_scatter(
            summed[0].astype(jnp.bfloat16), "dp", scatter_dimension=1, tiled=True
        ).astype(jnp.float32),
        lax.psum_scatter(
            summed[1].astype(jnp.bfloat16), "dp", scatter_dimension=0, tiled=True
        ).astype(jnp.float32),
    )
    return (next_input, sent_back, expand_grad[None], reduce_grad[None], filter_grad[None])


def solution(mesh):
    return jax.shard_map(
        on_device,
        mesh=mesh,
        in_specs=(
            P("pipe", "dp", "sp", None, None),
            P("pipe", "dp", "sp", None, None),
            P("pipe", "dp", "sp", None, None),
            P("pipe", None, None),
            P("pipe", None, None),
            P("pipe", None, None, None),
            P(),
        ),
        out_specs=(
            P("pipe", "dp", "sp", None, None),
            P("pipe", "dp", "sp", None, None),
            P("pipe", None, "dp"),
            P("pipe", "dp", None),
            P("pipe", None, None, None),
        ),
        check_vma=False,
    )
```

profile of v0, /device:TPU:0, one launch (start us, length us, event | category | flops | bytes accessed | tf_op | source)
XLA Modules:
  0.0 807.0 jit_solution(4464652124420981998)
XLA Ops:
  14.0 8.9 %copy.39 = bf16[2,60,2,120,128]{4,2,1,0,3:T(2,128)(2,1)} copy(bf16[2,60,2,120,128]{4,3,2,1,0:T(8,128)(2,1)S(1)} %bitcast.168) | data formatting | bytes 14745600 | tf_op jit(solution)/shard_map/reshape | solution.py:111
  30.1 240.9 %while.18 = (s32[]{:T(128)}, f32[60,120]{1,0:T(8,128)S(1)}, f32[60,120]{1,0:T(8,128)S(1)}, f32[120,60,120]{2,1,0:T(8,128)}, s32[120]{0:T(128)S(1)}, /*index=5*/f...) while((s32[]{:T(128)}, f32[60,120]{1,0:T(8,128)S(1)}, ...), condition=%wide.region_1.2_spmd.clone, body=%wide.region_0.1_spmd.clone.sunk | while | flops 65294 | bytes 151427 | solution.py:65
  280.1 7.4 copy.41
  287.5 12.1 %convolution_bitcast_fusion = f32[2,60,2,120,128]{4,3,2,0,1:T(8,128)} fusion(bf16[2,120,2,60,128]{4,2,3,1,0:T(2,128)(2,1)} %bitcast.162, bf16[60,120,120,1,1]{2,0,1,4,3:T(8,128)(2,1)S(1)} %get-tuple-element.230), kind=kOutput, calls=%fused_computation.24 | convolution fusion | flops 884736000 | bytes 23846400 | tf_op jit(solution)/shard_map/tlj,sjrtc->strlc/dot_general | solution.py:113
  299.6 8.6 %subtract_convert_fusion = (bf16[2,60,1,120,128]{4,3,2,0,1:T(8,128)(2,1)}, bf16[2,60,1,120,128]{4,3,2,0,1:T(8,128)(2,1)}) fusion(f32[2,60,2,120,128]{4,3,2,0,1:T(8,128)} %convolution_bitcast_fusion, f32[120,128]{1,0:T(8,128)S(1)} %get-tuple-element.234, f32[120,128]{1,0:T(8,128)S(1)} %get-tuple-element.233), kind=kLoop, calls=%fused_computation.48 | loop fusion | flops 14745600 | bytes 22241280 | tf_op jit(solution)/shard_map/convert.6
  308.2 11.1 %convert_bitcast_fusion = bf16[2,120,2,60,128]{4,1,2,0,3:T(8,128)(2,1)} fusion(bf16[2,60,1,120,128]{4,3,2,0,1:T(8,128)(2,1)} %get-tuple-element.220, bf16[2,60,1,120,128]{4,3,2,0,1:T(8,128)(2,1)} %get-tuple-element.219, bf16[60,120,120,1,1]{2,0,1,4,3:T(8,128)(2,1)S(1)} %copy-done.7), kind=kOutput, calls=%fused_computation.46 | convolution fusion | flops 892108800 | bytes 16473600 | tf_op jit(solution)/shard_map/tlj,strlc->sjrtc/dot_general | solution.py:117
  319.2 11.9 %copy.45 = bf16[2,120,2,60,128]{4,2,0,3,1:T(2,128)(2,1)} copy(bf16[2,120,2,60,128]{4,1,2,0,3:T(8,128)(2,1)} %convert_bitcast_fusion) | data formatting | bytes 14745600 | tf_op jit(solution)/shard_map/convert_element_type | solution.py:119
  337.8 9.4 %bitcast_multiply_fusion = bf16[14400,128]{1,0:T(8,128)(2,1)} fusion(bf16[1,1,60,240,128]{4,3,2,1,0:T(8,128)(2,1)} %param.11, bf16[14400]{0:T(1024)(128)(2,1)S(1)} %mul.489), kind=kLoop, calls=%fused_computation.58 | loop fusion | flops 1843200 | bytes 7401600 | tf_op jit(solution)/shard_map/mul | solution.py:138
  353.8 67.0 %all-to-all-done.1 = bf16[2,120,2,60,128]{4,2,0,3,1:T(2,128)(2,1)} async-done(((bf16[2,120,2,60,128]{4,2,0,3,1:T(2,128)(2,1)}), bf16[2,120,2,60,128]{4,2,0,3,1:T(2,128)(2,1)}, u32[]{:S(2)}, u32[]{:S(2)}) %all-to-all-start.1) | async-done | bytes 7372832 | tf_op jit(solution)/shard_map/all_to_all | solution.py:102
  420.9 11.0 %copy.47 = bf16[2,60,2,2,60,128]{5,0,4,3,2,1:T(2,128)(2,1)S(1)} copy(bf16[2,60,2,2,60,128]{5,2,0,4,1,3:T(2,128)(2,1)} %bitcast.25) | data formatting | bytes 14745600 | tf_op jit(solution)/shard_map/all_to_all | solution.py:102
  431.9 7.3 fusion.30
  439.2 12.9 %fusion.100 = (f32[1,60,240,128]{3,2,1,0:T(8,128)S(1)}, bf16[1,60,240,128]{3,2,1,0:T(8,128)(2,1)}, bf16[1,60,240,128]{3,2,1,0:T(8,128)(2,1)S(1)}, f32[1,60,240,128]{3,2,1,0:T(8,128)}) fusion(f32[2,60,240,128]{3,2,1,0:T(8,128)} %fusion.30, bf16[1,1,60,240,128]{4,3,2,1,0:T(8,128)(2,1)} %param.9, bf16[1,1,60,240,128]{4,3,2,1,0:T(8,128)(2,1)} %param.10), kind=kLoop, calls=%fused_computation.174 | loop fusion | flops 11059200 | bytes 44236800 | tf_op jit(solution)/shard_map/slice | solution.py:178
  455.8 17.0 %fusion.65 = f32[14400,768]{1,0:T(8,128)} fusion(bf16[14400,128]{1,0:T(8,128)(2,1)S(1)} %bitcast.163, bf16[1,128,768]{2,1,0:T(8,128)(2,1)S(1)} %copy-done), kind=kOutput, calls=%fused_computation.84 | convolution fusion | flops 2831155200 | bytes 48119808 | tf_op jit(solution)/shard_map/dot_general | solution.py:129
  472.9 30.9 %fusion.7 = bf16[14400,768]{1,0:T(8,128)(2,1)} fusion(f32[14400,768]{1,0:T(8,128)} %fusion.65, bf16[14400,128]{1,0:T(8,128)(2,1)} %bitcast.170, bf16[1,768,128]{2,1,0:T(8,128)(2,1)S(1)} %copy-done.20), kind=kOutput, calls=%fused_computation.14 | convolution fusion | flops 2941747200 | bytes 70238208 | tf_op jit(solution)/shard_map/dot_general | solution.py:140
  503.8 10.9 %convolution_add_fusion = f32[14400,128]{1,0:T(8,128)S(1)} fusion(bf16[14400,768]{1,0:T(8,128)(2,1)} %fusion.7, bf16[14400,128]{1,0:T(8,128)(2,1)S(1)} %copy-done.2, bf16[1,128,768]{2,1,0:T(8,128)(2,1)S(1)} %copy-done), kind=kOutput, calls=%fused_computation.22 | convolution fusion | flops 2834841600 | bytes 33374208 | tf_op jit(solution)/shard_map/dot_general | solution.py:143
  527.8 16.7 %fusion.11 = f32[14400,128]{1,0:T(8,128)} fusion(bf16[14400,128]{1,0:T(8,128)(2,1)} %bitcast.173, f32[14400,128]{1,0:T(8,128)} %bitcast.167, bf16[14400,128]{1,0:T(8,128)(2,1)} %bitcast.172, bf16[1,768,128]{2,1,0:T(8,128)(2,1)S(1)} %copy-done.20, bf16[1,128,768]{2,1,0:T(8,128)(2,1)S(1)} %copy-done), kind=kOutput, calls=%fused_computation.21 | convolution fusion | flops 5723136000 | bytes 22511616 | tf_op jit(solution)/shard_map/dot_general | solution.py:131
  553.3 16.1 %all-to-all-done.2 = bf16[60,2,120,128]{3,1,0,2:T(2,128)(2,1)} async-done(((bf16[60,2,120,128]{3,1,0,2:T(2,128)(2,1)}), bf16[60,2,120,128]{3,1,0,2:T(2,128)(2,1)}, u32[]{:S(2)}, u32[]{:S(2)}) %all-to-all-start.2) | async-done | bytes 3686432 | tf_op jit(solution)/shard_map/all_to_all | solution.py:194
  593.8 14.8 %convolution_convert_fusion = bf16[128,768]{0,1:T(8,128)(2,1)} fusion(bf16[14400,128]{1,0:T(8,128)(2,1)} %fusion.22, bf16[14400,768]{1,0:T(8,128)(2,1)} %fusion.7), kind=kOutput, calls=%fused_computation.76 | convolution fusion | flops 2831253504 | bytes 26001408 | tf_op jit(solution)/shard_map/dot_general | solution.py:142
  608.6 25.9 %all-to-all-done.3 = bf16[120,2,60,128]{3,1,2,0:T(2,128)(2,1)} async-done(((bf16[120,2,60,128]{3,1,2,0:T(2,128)(2,1)}), bf16[120,2,60,128]{3,1,2,0:T(2,128)(2,1)}, u32[]{:S(2)}, u32[]{:S(2)}) %all-to-all-start.3) | async-done | bytes 3686432 | tf_op jit(solution)/shard_map/all_to_all | solution.py:216
  646.2 7.4 fusion.36
  654.9 20.0 %fusion.57 = bf16[768,128]{1,0:T(8,128)(2,1)} fusion(bf16[14400,128]{1,0:T(8,128)(2,1)S(1)} %copy-done.3, f32[14400,768]{1,0:T(8,128)} %fusion.65), kind=kOutput, calls=%fused_computation.75 | convolution fusion | flops 2886549504 | bytes 48119808 | tf_op jit(solution)/shard_map/dot_general | solution.py:139
  675.0 22.3 %reduce-scatter.5.cloned.1.call-done = bf16[192,128]{1,0:T(8,128)(2,1)} async-done(((bf16[768,128]{1,0:T(8,128)(2,1)}), bf16[192,128]{1,0:T(8,128)(2,1)}) %reduce-scatter.5.cloned.1.call-update) | async-done | bytes 49168 | tf_op jit(solution)/shard_map/reduce_scatter | solution.py:236
  697.4 21.7 %all-reduce.6.cloned.1.call-done = (bf16[128,192]{0,1:T(8,128)(2,1)}, bf16[192,128]{1,0:T(8,128)(2,1)}) async-done(((bf16[128,192]{0,1:T(8,128)(2,1)}, bf16[192,128]{1,0:T(8,128)(2,1)}), (bf16[128,192]{0,1:T(8,128)(2,1)}, bf16[192,128]{1,0:T(8,128)(2,1)})) %all-reduce.6.cloned.1.call-update) | async-done | bytes 98320 | tf_op jit(solution)/shard_map/psum | solution.py:229
  722.7 68.0 %all-reduce.4.cloned.1.call-done = f32[1,2,120,128]{3,2,1,0:T(8,128)} async-done(((f32[1,2,120,128]{3,2,1,0:T(8,128)}), f32[1,2,120,128]{3,2,1,0:T(8,128)}) %all-reduce.4.cloned.1.call-update) | async-done | bytes 122896 | tf_op jit(solution)/shard_map/psum | solution.py:227
  (583 shorter events, 270.9 us)
Async XLA Ops:
  8.0 447.8 %copy-start = (bf16[1,128,768]{2,1,0:T(8,128)(2,1)S(1)}, bf16[1,128,768]{2,1,0:T(8,128)(2,1)}, u32[]{:S(2)}) copy-start(bf16[1,128,768]{2,1,0:T(8,128)(2,1)} %param.12) | copy-start | bytes 589828
  22.9 7.1 copy-start.19
  22.9 249.0 %copy-start.16 = (f32[1,2,120,128]{3,2,1,0:T(8,128)S(1)}, f32[1,2,120,128]{3,2,1,0:T(8,128)}, u32[]{:S(2)}) copy-start(f32[1,2,120,128]{3,2,1,0:T(8,128)} %param.14) | copy-start | bytes 368644
  22.9 257.3 %all-to-all-start = ((bf16[2,60,2,120,128]{4,2,1,0,3:T(2,128)(2,1)}), bf16[2,60,2,120,128]{4,2,1,0,3:T(2,128)(2,1)}, u32[]{:S(2)}, u32[]{:S(2)}) async-start(bf16[2,60,2,120,128]{4,2,1,0,3:T(2,128)(2,1)} %copy.39), calls=%async_computation | async-start | bytes 14745600 | tf_op jit(solution)/shard_map/all_to_all | solution.py:98
  271.9 27.8 %copy-start.8 = (f32[120,128]{1,0:T(8,128)}, f32[120,128]{1,0:T(8,128)S(1)}, u32[]{:S(2)}) copy-start(f32[120,128]{1,0:T(8,128)S(1)} %get-tuple-element.233) | copy-start | bytes 184324
  271.9 27.8 %copy-start.10 = (f32[120,128]{1,0:T(8,128)}, f32[120,128]{1,0:T(8,128)S(1)}, u32[]{:S(2)}) copy-start(f32[120,128]{1,0:T(8,128)S(1)} %get-tuple-element.234) | copy-start | bytes 184324
  299.6 8.6 %copy-start.7 = (bf16[60,120,120,1,1]{2,0,1,4,3:T(8,128)(2,1)S(1)}, bf16[60,120,120,1,1]{2,0,1,4,3:T(8,128)(2,1)}, u32[]{:S(2)}) copy-start(bf16[60,120,120,1,1]{2,0,1,4,3:T(8,128)(2,1)} %get-tuple-element.231) | copy-start | bytes 5184004
  331.1 89.7 %all-to-all-start.1 = ((bf16[2,120,2,60,128]{4,2,0,3,1:T(2,128)(2,1)}), bf16[2,120,2,60,128]{4,2,0,3,1:T(2,128)(2,1)}, u32[]{:S(2)}, u32[]{:S(2)}) async-start(bf16[2,120,2,60,128]{4,2,0,3,1:T(2,128)(2,1)} %copy.45), calls=%async_computation.1 | async-start | bytes 14745600 | tf_op jit(solution)/shard_map/all_to_all | solution.py:102
  455.8 17.1 %copy-start.20 = (bf16[1,768,128]{2,1,0:T(8,128)(2,1)S(1)}, bf16[1,768,128]{2,1,0:T(8,128)(2,1)}, u32[]{:S(2)}) copy-start(bf16[1,768,128]{2,1,0:T(8,128)(2,1)} %param.13) | copy-start | bytes 589828
  472.9 30.9 %copy-start.2 = (bf16[14400,128]{1,0:T(8,128)(2,1)S(1)}, bf16[14400,128]{1,0:T(8,128)(2,1)}, u32[]{:S(2)}) copy-start(bf16[14400,128]{1,0:T(8,128)(2,1)} %bitcast_multiply_fusion) | copy-start | bytes 11059204
  522.4 47.1 %all-to-all-start.2 = ((bf16[60,2,120,128]{3,1,0,2:T(2,128)(2,1)}), bf16[60,2,120,128]{3,1,0,2:T(2,128)(2,1)}, u32[]{:S(2)}, u32[]{:S(2)}) async-start(bf16[60,2,120,128]{3,1,0,2:T(2,128)(2,1)} %copy.50), calls=%async_computation.2 | async-start | bytes 7372800 | tf_op jit(solution)/shard_map/all_to_all | solution.py:194
  527.8 16.7 %copy-start.18 = (f32[60]{0:T(128)S(1)}, f32[60]{0:T(128)}, u32[]{:S(2)}) copy-start(f32[60]{0:T(128)} %get-tuple-element.212) | copy-start | bytes 724
  550.1 24.1 %copy-start.4 = (bf16[60,120,120,1]{2,0,1,3:T(8,128)(2,1)S(1)}, bf16[60,120,120,1]{2,0,1,3:T(8,128)(2,1)}, u32[]{:S(2)}) copy-start(bf16[60,120,120,1]{2,0,1,3:T(8,128)(2,1)} %get-tuple-element.232) | copy-start | bytes 5184004
  550.1 172.6 %collective-permute-start = (bf16[1,1,60,240,128]{4,3,2,1,0:T(8,128)(2,1)}, bf16[1,1,60,240,128]{4,3,2,1,0:T(8,128)(2,1)}, u32[]{:S(2)}, u32[]{:S(2)}) collective-permute-start(bf16[1,1,60,240,128]{4,3,2,1,0:T(8,128)(2,1)} %multiply_convert_fusion.6), channel_id=1, source_target_pairs={{0,8},{8,16},{16,24},{1,9},{9,17},{17,25},{2,10},{10,18},{18,26},{... | collective-permute-start | bytes 11059208 | tf_op jit(solution)/shard_map/ppermute | solution.py:16
  569.5 6.7 slice-start
  588.3 46.3 %all-to-all-start.3 = ((bf16[120,2,60,128]{3,1,2,0:T(2,128)(2,1)}), bf16[120,2,60,128]{3,1,2,0:T(2,128)(2,1)}, u32[]{:S(2)}, u32[]{:S(2)}) async-start(bf16[120,2,60,128]{3,1,2,0:T(2,128)(2,1)} %copy.56), calls=%async_computation.3 | async-start | bytes 7372800 | tf_op jit(solution)/shard_map/all_to_all | solution.py:216
  593.7 81.2 %reduce-scatter.3.cloned.1.call-start = ((), (), s32[]{:S(2)}) async-start(), calls=%async_computation.7 | async-start | bytes 245760 | tf_op jit(solution)/shard_map/reduce_scatter | solution.py:233
  608.6 88.7 %reduce-scatter.5.cloned.1.call-start = ((), (), s32[]{:S(2)}) async-start(), calls=%async_computation.8 | async-start | bytes 245760 | tf_op jit(solution)/shard_map/reduce_scatter | solution.py:236
  639.6 6.6 copy-start.13
  639.6 6.6 copy-start.15
  646.2 8.7 %copy-start.3 = (bf16[14400,128]{1,0:T(8,128)(2,1)S(1)}, bf16[14400,128]{1,0:T(8,128)(2,1)}, u32[]{:S(2)}) copy-start(bf16[14400,128]{1,0:T(8,128)(2,1)} %bitcast_multiply_fusion) | copy-start | bytes 11059204
  653.6 69.1 %collective-permute-start.1 = (bf16[1,1,60,240,128]{4,3,2,1,0:T(8,128)(2,1)}, bf16[1,1,60,240,128]{4,3,2,1,0:T(8,128)(2,1)}, u32[]{:S(2)}, u32[]{:S(2)}) collective-permute-start(bf16[1,1,60,240,128]{4,3,2,1,0:T(8,128)(2,1)} %fusion.36), channel_id=1, source_target_pairs={{8,0},{16,8},{24,16},{9,1},{17,9},{25,17},{10,2},{18,10},{26,18},{... | collective-permute-start | bytes 11059208 | tf_op jit(solution)/shard_map/ppermute | solution.py:16
  674.9 44.2 %all-reduce.6.cloned.1.call-start = ((), (), s32[]{:S(2)}) async-start(), calls=%async_computation.9 | async-start | bytes 196608 | tf_op jit(solution)/shard_map/psum | solution.py:229
  697.3 93.4 %all-reduce.4.cloned.1.call-start = ((), (), s32[]{:S(2)}) async-start(), calls=%async_computation.6 | async-start | bytes 245760 | tf_op jit(solution)/shard_map/psum | solution.py:227
  (9 other events, 31.1 us)
Sparse Core Ops, SparseCore 0:
  608.7 21.2 reduce-scatter.2
  675.0 22.2 reduce-scatter.4
  699.6 19.4 all-reduce.5
Sparse Core Ops, SparseCore 1:
  721.3 69.3 all-reduce.3
where the time goes:
time: 813 us; the launch traced here: 807 us
  waiting for transfers between devices  221 us (27%)
  matrix products  161 us (20%)
  local copies, waits for them, and re-layouts  153 us (19%)
  other arithmetic  146 us (18%)
  loops' own time  80.9 us (10%)
  starting transfers between devices  29.2 us (4%)
  between operations  15.8 us (2%)
    dynamic_update_slice x120, other arithmetic, legendre(): lax.scan(advance, (zero_rows, zero_rows), jnp.arange(cycles, dtype=jnp.in...  87.6 us
    another operation x1, loops' own time, legendre(): lax.scan(advance, (zero_rows, zero_rows), jnp.arange(cycles, dtype=jnp.in...  80.9 us
    dynamic_slice x120, local copies, waits for them, and re-layouts, legendre(): lax.scan(advance, (zero_rows, zero_rows), jnp.arange(cycles, dtype=jnp.in...  69.9 us
    psum x1, waiting for transfers between devices, on_device(): filter_grad = lax.psum(jnp.stack([filter_real, filter_imag]), ('sp', 'dp'))  68 us
    all_to_all x1, waiting for transfers between devices, joint_cycles(): return lax.all_to_all(values, 'sp', split_axis=1, concat_axis=3, tiled=True)  67 us
    dot_general x1, matrix products, backward_rows(): jnp.dot(masked, contract.T, preferred_element_type=jnp.float32)  30.9 us
    all_to_all x1, waiting for transfers between devices, on_device(): lax.all_to_all(grad_coeffs, 'sp', split_axis=0, concat_axis=2, tiled=True)  25.9 us
    reduce_scatter x1, waiting for transfers between devices, on_device(): lax.psum_scatter(summed[1].astype(jnp.bfloat16), 'dp', scatter_dimension=...  22.3 us
  transfers between devices with their start and end apart: 10, of which 6 were waited for; matrix products, arithmetic and copies ran while one was open for 35% of the time, Pallas kernels for 0%

commit v1 on v0

--- a/solution.py
+++ b/solution.py
@@ -224,7 +224,9 @@
         (grad_mixed.reshape(grid_shape) + grad_tokens) * cycle_mask[:, None, None]
     ).astype(jnp.bfloat16)
     sent_back = from_behind(input_grad[None, None], "pipe", -1)
-    filter_grad = lax.psum(jnp.stack([filter_real, filter_imag]), ("sp", "dp"))
+    filter_grad = jnp.sum(
+        lax.all_gather(jnp.stack([filter_real, filter_imag]), ("sp", "dp")), axis=0
+    )
     summed = (
         lax.psum(grad_expand.astype(jnp.bfloat16), "sp").astype(jnp.float32),
         lax.psum(grad_reduce.astype(jnp.bfloat16), "sp").astype(jnp.float32),

time: 813 us -> 777 us (0.956)
  waiting for transfers between devices: 221 us -> 153 us
  blocking collectives: 0 us -> 34.4 us
    psum x1 -> x0, waiting for transfers between devices: 68 us -> none  [on_device(): filter_grad = lax.psum(jnp.stack([filter_real, filter_imag]), ('sp', 'dp'))]
    all_gather x0 -> x1, blocking collectives: none -> 34.4 us  [on_device(): lax.all_gather(jnp.stack([filter_real, filter_imag]), ('sp', 'dp'))]
  transfers between devices with their start and end apart: 10 -> 9, of which waited for: 6 -> 5; matrix products, arithmetic and copies ran while one was open for 35% -> 37% of each run, Pallas kernels for 0% -> 0%
where the time goes in v1:
time: 777 us; the launch traced here: 771 us
  matrix products  161 us (21%)
  waiting for transfers between devices  153 us (20%)
  local copies, waits for them, and re-layouts  152 us (20%)
  other arithmetic  146 us (19%)
  loops' own time  80.9 us (10%)
  blocking collectives  34.4 us (4%)
  starting transfers between devices  29.1 us (4%)
  between operations  14.4 us (2%)
    dynamic_update_slice x120, other arithmetic, legendre(): lax.scan(advance, (zero_rows, zero_rows), jnp.arange(cycles, dtype=jnp.in...  87.6 us
    another operation x1, loops' own time, legendre(): lax.scan(advance, (zero_rows, zero_rows), jnp.arange(cycles, dtype=jnp.in...  80.9 us
    dynamic_slice x120, local copies, waits for them, and re-layouts, legendre(): lax.scan(advance, (zero_rows, zero_rows), jnp.arange(cycles, dtype=jnp.in...  69.9 us
    all_to_all x1, waiting for transfers between devices, joint_cycles(): return lax.all_to_all(values, 'sp', split_axis=1, concat_axis=3, tiled=True)  67 us
    all_gather x1, blocking collectives, on_device(): lax.all_gather(jnp.stack([filter_real, filter_imag]), ('sp', 'dp'))  34.4 us
    dot_general x1, matrix products, backward_rows(): jnp.dot(masked, contract.T, preferred_element_type=jnp.float32)  31 us
    all_to_all x1, waiting for transfers between devices, on_device(): lax.all_to_all(grad_coeffs, 'sp', split_axis=0, concat_axis=2, tiled=True)  25.9 us
    reduce_scatter x1, waiting for transfers between devices, on_device(): lax.psum_scatter(summed[1].astype(jnp.bfloat16), 'dp', scatter_dimension=...  22.3 us
  transfers between devices with their start and end apart: 9, of which 5 were waited for; matrix products, arithmetic and copies ran while one was open for 37% of the time, Pallas kernels for 0%

profile of v1, /device:TPU:0, one launch (start us, length us, event | category | flops | bytes accessed | tf_op | source)
XLA Modules:
  0.0 771.5 jit_solution(3760414547476445550)
XLA Ops:
  13.2 8.8 %copy.39 = bf16[2,60,2,120,128]{4,2,1,0,3:T(2,128)(2,1)} copy(bf16[2,60,2,120,128]{4,3,2,1,0:T(8,128)(2,1)S(1)} %bitcast.168) | data formatting | bytes 14745600 | tf_op jit(solution)/shard_map/reshape | solution.py:111
  29.2 240.9 %while.18 = (s32[]{:T(128)}, f32[60,120]{1,0:T(8,128)S(1)}, f32[60,120]{1,0:T(8,128)S(1)}, f32[120,60,120]{2,1,0:T(8,128)}, s32[120]{0:T(128)S(1)}, /*index=5*/f...) while((s32[]{:T(128)}, f32[60,120]{1,0:T(8,128)S(1)}, ...), condition=%wide.region_1.2_spmd.clone, body=%wide.region_0.1_spmd.clone.sunk | while | flops 65294 | bytes 151427 | solution.py:65
  279.4 7.4 copy.41
  286.8 12.1 %convolution_bitcast_fusion = f32[2,60,2,120,128]{4,3,2,0,1:T(8,128)} fusion(bf16[2,120,2,60,128]{4,2,3,1,0:T(2,128)(2,1)} %bitcast.162, bf16[60,120,120,1,1]{2,0,1,4,3:T(8,128)(2,1)S(1)} %get-tuple-element.230), kind=kOutput, calls=%fused_computation.24 | convolution fusion | flops 884736000 | bytes 23846400 | tf_op jit(solution)/shard_map/tlj,sjrtc->strlc/dot_general | solution.py:113
  298.9 8.6 %subtract_convert_fusion = (bf16[2,60,1,120,128]{4,3,2,0,1:T(8,128)(2,1)}, bf16[2,60,1,120,128]{4,3,2,0,1:T(8,128)(2,1)}) fusion(f32[2,60,2,120,128]{4,3,2,0,1:T(8,128)} %convolution_bitcast_fusion, f32[120,128]{1,0:T(8,128)S(1)} %get-tuple-element.234, f32[120,128]{1,0:T(8,128)S(1)} %get-tuple-element.233), kind=kLoop, calls=%fused_computation.48 | loop fusion | flops 14745600 | bytes 22241280 | tf_op jit(solution)/shard_map/convert.6
  307.5 11.1 %convert_bitcast_fusion = bf16[2,120,2,60,128]{4,1,2,0,3:T(8,128)(2,1)} fusion(bf16[2,60,1,120,128]{4,3,2,0,1:T(8,128)(2,1)} %get-tuple-element.220, bf16[2,60,1,120,128]{4,3,2,0,1:T(8,128)(2,1)} %get-tuple-element.219, bf16[60,120,120,1,1]{2,0,1,4,3:T(8,128)(2,1)S(1)} %copy-done.7), kind=kOutput, calls=%fused_computation.46 | convolution fusion | flops 892108800 | bytes 16473600 | tf_op jit(solution)/shard_map/tlj,strlc->sjrtc/dot_general | solution.py:117
  318.5 11.9 %copy.45 = bf16[2,120,2,60,128]{4,2,0,3,1:T(2,128)(2,1)} copy(bf16[2,120,2,60,128]{4,1,2,0,3:T(8,128)(2,1)} %convert_bitcast_fusion) | data formatting | bytes 14745600 | tf_op jit(solution)/shard_map/convert_element_type | solution.py:119
  337.1 9.4 %bitcast_multiply_fusion = bf16[14400,128]{1,0:T(8,128)(2,1)} fusion(bf16[1,1,60,240,128]{4,3,2,1,0:T(8,128)(2,1)} %param.11, bf16[14400]{0:T(1024)(128)(2,1)S(1)} %mul.489), kind=kLoop, calls=%fused_computation.58 | loop fusion | flops 1843200 | bytes 7401600 | tf_op jit(solution)/shard_map/mul | solution.py:138
  353.1 67.0 %all-to-all-done.1 = bf16[2,120,2,60,128]{4,2,0,3,1:T(2,128)(2,1)} async-done(((bf16[2,120,2,60,128]{4,2,0,3,1:T(2,128)(2,1)}), bf16[2,120,2,60,128]{4,2,0,3,1:T(2,128)(2,1)}, u32[]{:S(2)}, u32[]{:S(2)}) %all-to-all-start.1) | async-done | bytes 7372832 | tf_op jit(solution)/shard_map/all_to_all | solution.py:102
  420.1 11.0 %copy.47 = bf16[2,60,2,2,60,128]{5,0,4,3,2,1:T(2,128)(2,1)S(1)} copy(bf16[2,60,2,2,60,128]{5,2,0,4,1,3:T(2,128)(2,1)} %bitcast.25) | data formatting | bytes 14745600 | tf_op jit(solution)/shard_map/all_to_all | solution.py:102
  431.1 7.3 fusion.30
  438.5 12.9 %fusion.100 = (f32[1,60,240,128]{3,2,1,0:T(8,128)S(1)}, bf16[1,60,240,128]{3,2,1,0:T(8,128)(2,1)}, bf16[1,60,240,128]{3,2,1,0:T(8,128)(2,1)S(1)}, f32[1,60,240,128]{3,2,1,0:T(8,128)}) fusion(f32[2,60,240,128]{3,2,1,0:T(8,128)} %fusion.30, bf16[1,1,60,240,128]{4,3,2,1,0:T(8,128)(2,1)} %param.9, bf16[1,1,60,240,128]{4,3,2,1,0:T(8,128)(2,1)} %param.10), kind=kLoop, calls=%fused_computation.174 | loop fusion | flops 11059200 | bytes 44236800 | tf_op jit(solution)/shard_map/slice | solution.py:178
  455.1 17.1 %fusion.65 = f32[14400,768]{1,0:T(8,128)} fusion(bf16[14400,128]{1,0:T(8,128)(2,1)S(1)} %bitcast.163, bf16[1,128,768]{2,1,0:T(8,128)(2,1)S(1)} %copy-done), kind=kOutput, calls=%fused_computation.84 | convolution fusion | flops 2831155200 | bytes 48119808 | tf_op jit(solution)/shard_map/dot_general | solution.py:129
  472.1 31.0 %fusion.7 = bf16[14400,768]{1,0:T(8,128)(2,1)} fusion(f32[14400,768]{1,0:T(8,128)} %fusion.65, bf16[14400,128]{1,0:T(8,128)(2,1)} %bitcast.171, bf16[1,768,128]{2,1,0:T(8,128)(2,1)S(1)} %copy-done.19), kind=kOutput, calls=%fused_computation.14 | convolution fusion | flops 2941747200 | bytes 70238208 | tf_op jit(solution)/shard_map/dot_general | solution.py:140
  503.1 10.9 %convolution_add_fusion = f32[14400,128]{1,0:T(8,128)S(1)} fusion(bf16[14400,768]{1,0:T(8,128)(2,1)} %fusion.7, bf16[14400,128]{1,0:T(8,128)(2,1)S(1)} %copy-done.2, bf16[1,128,768]{2,1,0:T(8,128)(2,1)S(1)} %copy-done), kind=kOutput, calls=%fused_computation.22 | convolution fusion | flops 2834841600 | bytes 33374208 | tf_op jit(solution)/shard_map/dot_general | solution.py:143
  527.1 16.7 %fusion.11 = f32[14400,128]{1,0:T(8,128)} fusion(bf16[14400,128]{1,0:T(8,128)(2,1)} %bitcast.174, f32[14400,128]{1,0:T(8,128)} %bitcast.167, bf16[14400,128]{1,0:T(8,128)(2,1)} %bitcast.173, bf16[1,768,128]{2,1,0:T(8,128)(2,1)S(1)} %copy-done.19, bf16[1,128,768]{2,1,0:T(8,128)(2,1)S(1)} %copy-done), kind=kOutput, calls=%fused_computation.21 | convolution fusion | flops 5723136000 | bytes 22511616 | tf_op jit(solution)/shard_map/dot_general | solution.py:131
  552.6 16.1 %all-to-all-done.2 = bf16[60,2,120,128]{3,1,0,2:T(2,128)(2,1)} async-done(((bf16[60,2,120,128]{3,1,0,2:T(2,128)(2,1)}), bf16[60,2,120,128]{3,1,0,2:T(2,128)(2,1)}, u32[]{:S(2)}, u32[]{:S(2)}) %all-to-all-start.2) | async-done | bytes 3686432 | tf_op jit(solution)/shard_map/all_to_all | solution.py:194
  593.1 14.8 %convolution_convert_fusion = bf16[128,768]{0,1:T(8,128)(2,1)} fusion(bf16[14400,128]{1,0:T(8,128)(2,1)} %fusion.22, bf16[14400,768]{1,0:T(8,128)(2,1)} %fusion.7), kind=kOutput, calls=%fused_computation.76 | convolution fusion | flops 2831253504 | bytes 26001408 | tf_op jit(solution)/shard_map/dot_general | solution.py:142
  607.9 25.9 %all-to-all-done.3 = bf16[120,2,60,128]{3,1,2,0:T(2,128)(2,1)} async-done(((bf16[120,2,60,128]{3,1,2,0:T(2,128)(2,1)}), bf16[120,2,60,128]{3,1,2,0:T(2,128)(2,1)}, u32[]{:S(2)}, u32[]{:S(2)}) %all-to-all-start.3) | async-done | bytes 3686432 | tf_op jit(solution)/shard_map/all_to_all | solution.py:216
  645.5 7.3 fusion.36
  654.2 20.1 %fusion.57 = bf16[768,128]{1,0:T(8,128)(2,1)} fusion(bf16[14400,128]{1,0:T(8,128)(2,1)S(1)} %copy-done.3, f32[14400,768]{1,0:T(8,128)} %fusion.65), kind=kOutput, calls=%fused_computation.75 | convolution fusion | flops 2886549504 | bytes 48119808 | tf_op jit(solution)/shard_map/dot_general | solution.py:139
  674.3 22.3 %reduce-scatter.5.cloned.1.call-done = bf16[192,128]{1,0:T(8,128)(2,1)} async-done(((bf16[768,128]{1,0:T(8,128)(2,1)}), bf16[192,128]{1,0:T(8,128)(2,1)}) %reduce-scatter.5.cloned.1.call-update) | async-done | bytes 49168 | tf_op jit(solution)/shard_map/reduce_scatter | solution.py:238
  696.7 21.8 %all-reduce.3.cloned.1.call-done = (bf16[128,192]{0,1:T(8,128)(2,1)}, bf16[192,128]{1,0:T(8,128)(2,1)}) async-done(((bf16[128,192]{0,1:T(8,128)(2,1)}, bf16[192,128]{1,0:T(8,128)(2,1)}), (bf16[128,192]{0,1:T(8,128)(2,1)}, bf16[192,128]{1,0:T(8,128)(2,1)})) %all-reduce.3.cloned.1.call-update) | async-done | bytes 98320 | tf_op jit(solution)/shard_map/psum | solution.py:231
  721.3 34.4 %all-gather = f32[16,120,128]{2,1,0:T(8,128)S(1)} all-gather(f32[2,120,128]{2,1,0:T(8,128)S(1)} %pad_maximum_fusion.2), channel_id=2, replica_groups=mesh['pipe'=4,'sp'=2,'dp'=4] {'sp','dp'}, dimensions={0}, use_global_device_ids=true | all-gather | bytes 1105920 | tf_op jit(solution)/shard_map/all_gather | solution.py:228
  (579 shorter events, 270.4 us)
Async XLA Ops:
  7.2 447.9 %copy-start = (bf16[1,128,768]{2,1,0:T(8,128)(2,1)S(1)}, bf16[1,128,768]{2,1,0:T(8,128)(2,1)}, u32[]{:S(2)}) copy-start(bf16[1,128,768]{2,1,0:T(8,128)(2,1)} %param.12) | copy-start | bytes 589828
  7.8 5.3 copy-start.12
  22.0 7.1 copy-start.18
  22.0 249.1 %copy-start.16 = (f32[1,2,120,128]{3,2,1,0:T(8,128)S(1)}, f32[1,2,120,128]{3,2,1,0:T(8,128)}, u32[]{:S(2)}) copy-start(f32[1,2,120,128]{3,2,1,0:T(8,128)} %param.14) | copy-start | bytes 368644
  22.0 257.4 %all-to-all-start = ((bf16[2,60,2,120,128]{4,2,1,0,3:T(2,128)(2,1)}), bf16[2,60,2,120,128]{4,2,1,0,3:T(2,128)(2,1)}, u32[]{:S(2)}, u32[]{:S(2)}) async-start(bf16[2,60,2,120,128]{4,2,1,0,3:T(2,128)(2,1)} %copy.39), calls=%async_computation | async-start | bytes 14745600 | tf_op jit(solution)/shard_map/all_to_all | solution.py:98
  271.1 27.8 %copy-start.8 = (f32[120,128]{1,0:T(8,128)}, f32[120,128]{1,0:T(8,128)S(1)}, u32[]{:S(2)}) copy-start(f32[120,128]{1,0:T(8,128)S(1)} %get-tuple-element.233) | copy-start | bytes 184324
  271.1 27.8 %copy-start.10 = (f32[120,128]{1,0:T(8,128)}, f32[120,128]{1,0:T(8,128)S(1)}, u32[]{:S(2)}) copy-start(f32[120,128]{1,0:T(8,128)S(1)} %get-tuple-element.234) | copy-start | bytes 184324
  298.9 8.6 %copy-start.7 = (bf16[60,120,120,1,1]{2,0,1,4,3:T(8,128)(2,1)S(1)}, bf16[60,120,120,1,1]{2,0,1,4,3:T(8,128)(2,1)}, u32[]{:S(2)}) copy-start(bf16[60,120,120,1,1]{2,0,1,4,3:T(8,128)(2,1)} %get-tuple-element.231) | copy-start | bytes 5184004
  330.4 89.7 %all-to-all-start.1 = ((bf16[2,120,2,60,128]{4,2,0,3,1:T(2,128)(2,1)}), bf16[2,120,2,60,128]{4,2,0,3,1:T(2,128)(2,1)}, u32[]{:S(2)}, u32[]{:S(2)}) async-start(bf16[2,120,2,60,128]{4,2,0,3,1:T(2,128)(2,1)} %copy.45), calls=%async_computation.1 | async-start | bytes 14745600 | tf_op jit(solution)/shard_map/all_to_all | solution.py:102
  455.1 17.1 %copy-start.19 = (bf16[1,768,128]{2,1,0:T(8,128)(2,1)S(1)}, bf16[1,768,128]{2,1,0:T(8,128)(2,1)}, u32[]{:S(2)}) copy-start(bf16[1,768,128]{2,1,0:T(8,128)(2,1)} %param.13) | copy-start | bytes 589828
  472.1 31.0 %copy-start.2 = (bf16[14400,128]{1,0:T(8,128)(2,1)S(1)}, bf16[14400,128]{1,0:T(8,128)(2,1)}, u32[]{:S(2)}) copy-start(bf16[14400,128]{1,0:T(8,128)(2,1)} %bitcast_multiply_fusion) | copy-start | bytes 11059204
  521.7 47.1 %all-to-all-start.2 = ((bf16[60,2,120,128]{3,1,0,2:T(2,128)(2,1)}), bf16[60,2,120,128]{3,1,0,2:T(2,128)(2,1)}, u32[]{:S(2)}, u32[]{:S(2)}) async-start(bf16[60,2,120,128]{3,1,0,2:T(2,128)(2,1)} %copy.50), calls=%async_computation.2 | async-start | bytes 7372800 | tf_op jit(solution)/shard_map/all_to_all | solution.py:194
  527.1 16.7 %copy-start.17 = (f32[60]{0:T(128)S(1)}, f32[60]{0:T(128)}, u32[]{:S(2)}) copy-start(f32[60]{0:T(128)} %get-tuple-element.212) | copy-start | bytes 724
  549.3 24.1 %copy-start.4 = (bf16[60,120,120,1]{2,0,1,3:T(8,128)(2,1)S(1)}, bf16[60,120,120,1]{2,0,1,3:T(8,128)(2,1)}, u32[]{:S(2)}) copy-start(bf16[60,120,120,1]{2,0,1,3:T(8,128)(2,1)} %get-tuple-element.232) | copy-start | bytes 5184004
  549.4 207.1 %collective-permute-start = (bf16[1,1,60,240,128]{4,3,2,1,0:T(8,128)(2,1)}, bf16[1,1,60,240,128]{4,3,2,1,0:T(8,128)(2,1)}, u32[]{:S(2)}, u32[]{:S(2)}) collective-permute-start(bf16[1,1,60,240,128]{4,3,2,1,0:T(8,128)(2,1)} %multiply_convert_fusion.6), channel_id=1, source_target_pairs={{0,8},{8,16},{16,24},{1,9},{9,17},{17,25},{2,10},{10,18},{18,26},{... | collective-permute-start | bytes 11059208 | tf_op jit(solution)/shard_map/ppermute | solution.py:16
  568.7 6.7 slice-start
  587.6 46.3 %all-to-all-start.3 = ((bf16[120,2,60,128]{3,1,2,0:T(2,128)(2,1)}), bf16[120,2,60,128]{3,1,2,0:T(2,128)(2,1)}, u32[]{:S(2)}, u32[]{:S(2)}) async-start(bf16[120,2,60,128]{3,1,2,0:T(2,128)(2,1)} %copy.56), calls=%async_computation.3 | async-start | bytes 7372800 | tf_op jit(solution)/shard_map/all_to_all | solution.py:216
  593.0 81.3 %reduce-scatter.3.cloned.1.call-start = ((), (), s32[]{:S(2)}) async-start(), calls=%async_computation.6 | async-start | bytes 245760 | tf_op jit(solution)/shard_map/reduce_scatter | solution.py:235
  607.9 88.8 %reduce-scatter.5.cloned.1.call-start = ((), (), s32[]{:S(2)}) async-start(), calls=%async_computation.7 | async-start | bytes 245760 | tf_op jit(solution)/shard_map/reduce_scatter | solution.py:238
  638.9 6.6 copy-start.13
  638.9 6.6 copy-start.15
  645.5 8.6 %copy-start.3 = (bf16[14400,128]{1,0:T(8,128)(2,1)S(1)}, bf16[14400,128]{1,0:T(8,128)(2,1)}, u32[]{:S(2)}) copy-start(bf16[14400,128]{1,0:T(8,128)(2,1)} %bitcast_multiply_fusion) | copy-start | bytes 11059204
  652.9 103.6 %collective-permute-start.1 = (bf16[1,1,60,240,128]{4,3,2,1,0:T(8,128)(2,1)}, bf16[1,1,60,240,128]{4,3,2,1,0:T(8,128)(2,1)}, u32[]{:S(2)}, u32[]{:S(2)}) collective-permute-start(bf16[1,1,60,240,128]{4,3,2,1,0:T(8,128)(2,1)} %fusion.36), channel_id=1, source_target_pairs={{8,0},{16,8},{24,16},{9,1},{17,9},{25,17},{10,2},{18,10},{26,18},{... | collective-permute-start | bytes 11059208 | tf_op jit(solution)/shard_map/ppermute | solution.py:16
  674.3 44.2 %all-reduce.3.cloned.1.call-start = ((), (), s32[]{:S(2)}) async-start(), calls=%async_computation.8 | async-start | bytes 196608 | tf_op jit(solution)/shard_map/psum | solution.py:231
  (7 other events, 21.6 us)
Sparse Core Ops, SparseCore 0:
  608.0 21.2 reduce-scatter.2
  674.4 22.2 reduce-scatter.4
  699.0 19.4 all-reduce.2
